TPU v7x, 512 devices: a whole 4x4x16 slice. The times are simulated.
512 devices in a mesh: row: 16 (over x, y), col: 32 (over z, core).
Axes of the slice: x: 4, y: 4, z: 16, core: 2. Of those that a mesh axis runs over, the one named last changes fastest.
Arguments:
- positions: float32 [3, 32768], P(None, ('row', 'col')), may hold values from -1 to 96, as said below
- noise: float32 [8, 3, 32768], P(None, None, ('row', 'col')), may hold values from -6 to 6
Outputs:
- basis: float32 [8, 3, 32768], P(None, None, ('row', 'col'))
- residual: float32 [8, 3, 32768], P(None, None, ('row', 'col'))
- coefficients: float32 [3, 8, 8], replicated
Inputs may be any that keep to these rules, and one draw needn't show every extreme that they name: `positions`: bead k lies within 0.77 of each coordinate of its own point of a cubic lattice of spacing 2.2 with 32 by 32 points a layer, distinct beads on distinct points.
All inputs are finite; a program needn't handle non-finite values.
Results may differ from a plain program's by a relative error of at most 0.0003.
Values sent between devices are 32-bit elements; how exact they have to be, the bound alone decides.
A program may use at most 64 MiB of HBM per device.

v0:
```python
import jax
import jax.numpy as jnp
from jax import lax
from jax.sharding import PartitionSpec as P


def pair_tensor(target_pos, source_pos):
    displace = target_pos[:, :, None] - source_pos[:, None, :]
    distance_sq = jnp.sum(displace * displace, axis=0)
    distance = jnp.sqrt(distance_sq)
    safe_distance = jnp.where(distance > 0, distance, 1.0)
    safe_sq = safe_distance * safe_distance
    far_iso = 0.75 / safe_distance * (1.0 + 2.0 / (3.0 * safe_sq))
    far_dir = 0.75 / safe_distance * (1.0 - 2.0 / safe_sq) / safe_sq
    near_iso = 1.0 - 9.0 * distance / 32.0
    near_dir = 3.0 / (32.0 * safe_distance)
    intersecting = distance < 2.0
    iso_part = jnp.where(intersecting, near_iso, far_iso)
    dir_part = jnp.where(intersecting, near_dir, far_dir)
    identity = jnp.eye(3, dtype=displace.dtype)
    return identity[:, :, None, None] * iso_part + dir_part * displace[:, None] * displace[None, :]


def local_gram(left, right):
    return jnp.einsum("kan,jan->kj", left, right, precision=lax.Precision.HIGHEST)


def combine(vectors, matrix):
    return jnp.einsum("kan,kj->jan", vectors, matrix, precision=lax.Precision.HIGHEST)


def lower_inverse(factor):
    return jax.scipy.linalg.solve_triangular(
        factor, jnp.eye(factor.shape[0], dtype=factor.dtype), lower=True
    )


def local(positions, noise):
    local_beads = positions.shape[1]
    total_count = 3.0 * local_beads * lax.axis_size("row") * lax.axis_size("col")
    target_pos = lax.all_gather(positions, "row", axis=1, tiled=True)
    source_pos = lax.all_gather(positions, "col", axis=1, tiled=True)

    def mobility(vectors):
        initial = jnp.zeros((vectors.shape[0], 3, target_pos.shape[1]), jnp.float32)
        source_piece = lax.all_gather(vectors, "col", axis=2, tiled=True)
        piece_width = source_piece.shape[2]
        block_count = 1
        while piece_width % block_count != 0 or piece_width // block_count > 256:
            block_count = block_count + 1
        block_width = piece_width // block_count

        def add_block(block_index, running):
            block_pos = lax.dynamic_slice_in_dim(
                source_pos, block_index * block_width, block_width, 1
            )
            block_vectors = lax.dynamic_slice_in_dim(
                source_piece, block_index * block_width, block_width, 2
            )
            tensor = pair_tensor(target_pos, block_pos)
            return running + jnp.einsum(
                "abts,kbs->kat", tensor, block_vectors, precision=lax.Precision.HIGHEST
            )

        partial_image = lax.fori_loop(0, block_count, add_block, initial)
        summed = lax.psum(partial_image, "row")
        return lax.dynamic_slice_in_dim(summed, lax.axis_index("row") * local_beads, local_beads, 2)

    start_matrix = lax.psum(local_gram(noise, noise), ("row", "col")) / total_count
    start_factor = jnp.linalg.cholesky(start_matrix)
    first = combine(noise, lower_inverse(start_factor).T)
    image = mobility(first)
    alpha_one = lax.psum(local_gram(first, image), ("row", "col")) / total_count
    remainder = image - combine(first, alpha_one)
    residual_matrix = lax.psum(local_gram(remainder, remainder), ("row", "col")) / total_count
    factor_one = jnp.linalg.cholesky(residual_matrix)
    basis = combine(remainder, lower_inverse(factor_one).T)
    image = mobility(basis) - combine(first, factor_one)
    alpha_two = lax.psum(local_gram(basis, image), ("row", "col")) / total_count
    residual = image - combine(basis, alpha_two)
    return (basis, residual, jnp.stack([alpha_one, factor_one, alpha_two]))


def solution(mesh):
    return jax.shard_map(
        local,
        mesh=mesh,
        in_specs=(P(None, ("row", "col")), P(None, None, ("row", "col"))),
        out_specs=(P(None, None, ("row", "col")), P(None, None, ("row", "col")), P()),
        check_vma=False,
    )
```

profile of v0, /device:TPU:1, one launch (start us, length us, event | category | flops | bytes accessed | tf_op | source)
XLA Modules:
  0.0 1041.4 jit_solution(14341036072423276544)
XLA Ops:
  7.2 38.0 %all-gather.1 = f32[32,64,3]{1,2,0:T(4,128)S(1)} all-gather(f32[1,64,3]{1,2,0:T(4,128)} %bitcast.96), channel_id=1, replica_groups=mesh['row'=16,'col'=32] {'col'}, dimensions={0}, use_global_device_ids=true | all-gather | bytes 25344 | tf_op jit(solution)/shard_map/all_gather | solution.py:42
  45.2 18.3 %all-gather = f32[16,64,3]{1,2,0:T(4,128)S(1)} all-gather(f32[1,64,3]{1,2,0:T(4,128)} %bitcast.97), channel_id=1, replica_groups=mesh['row'=16,'col'=32] {'row'}, dimensions={0}, use_global_device_ids=true | all-gather | bytes 13056 | tf_op jit(solution)/shard_map/all_gather | solution.py:41
  63.7 104.2 %psum.42 = f32[8,8]{0,1:T(8,128)S(1)} all-reduce(f32[8,8]{0,1:T(8,128)S(1)} %convolution_bitcast_fusion.5), channel_id=1, replica_groups=mesh['row'=16,'col'=32] {'row','col'}, use_global_device_ids=true, to_apply=%region_0.0 | all-reduce | flops 64 | bytes 512 | tf_op jit(solution)/shard_map/psum | solution.py:69
  171.1 44.3 %all_gather.12 = f32[8,3,2048]{0,1,2:T(4,128)} all-gather(f32[8,3,64]{0,1,2:T(4,128)S(1)} %copy.36), channel_id=1, replica_groups=mesh['row'=16,'col'=32] {'col'}, dimensions={2}, use_global_device_ids=true | all-gather | bytes 202752 | tf_op jit(solution)/shard_map/all_gather | solution.py:46
  215.4 3.3 copy.39
  218.9 120.9 %while.32 = (s32[]{:T(128)}, f32[8,3,1024]{2,0,1:T(8,128)S(1)}, f32[8,3,2048]{2,0,1:T(8,128)S(1)}, f32[3,1024]{1,0:T(4,128)S(1)}, f32[3,2048]{1,0:T(4,128)S(1)},...) while((s32[]{:T(128)}, f32[8,3,1024]{2,0,1:T(8,128)S(1)}, f32[8,3,2048]{2,0,1:T(8,128)S(1)}, ...), condition=%wide.region_5.8_spmd.clone, body=%wide.region_3.7_spmd.clone.sunk | while | flops 242270240 | bytes 19134656 | solution.py:65
  219.4 2.0 multiply_select_fusion.4
  221.4 2.1 subtract_multiply_fusion.4
  223.5 10.5 %fusion.87 = f32[8,3,1024]{2,0,1:T(8,128)S(1)} fusion(f32[3,1024,256]{2,1,0:T(8,128)} %get-tuple-element.423, f32[3,1024,256]{2,1,0:T(8,128)S(1)} %get-tuple-element.424, f32[1024,256]{1,0:T(8,128)} %get-tuple-element.425, f32[3,3]{1,0:T(4,128)S(1)} %fusion.86, f32[8,3,1024]{2,0,1:T(8,128)S(1)} %get-tuple-element.445, pred[]{:T(512)S(6)} %compare.14, ...), kind=kOutput, calls=%fused_computation.13.clone.1 | convolution fusion | flops 233619456 | bytes 7563269 | tf_op jit(solution)/shard_map/while/body/eval_jaxpr/abts,kbs->kat/dot_general | solution.py:61
  234.5 2.0 multiply_select_fusion.4
  236.5 2.1 subtract_multiply_fusion.4
  238.7 10.5 %fusion.87 = f32[8,3,1024]{2,0,1:T(8,128)S(1)} fusion(f32[3,1024,256]{2,1,0:T(8,128)} %get-tuple-element.423, f32[3,1024,256]{2,1,0:T(8,128)S(1)} %get-tuple-element.424, f32[1024,256]{1,0:T(8,128)} %get-tuple-element.425, f32[3,3]{1,0:T(4,128)S(1)} %fusion.86, f32[8,3,1024]{2,0,1:T(8,128)S(1)} %get-tuple-element.445, pred[]{:T(512)S(6)} %compare.14, ...), kind=kOutput, calls=%fused_computation.13.clone.1 | convolution fusion | flops 233619456 | bytes 7563269 | tf_op jit(solution)/shard_map/while/body/eval_jaxpr/abts,kbs->kat/dot_general | solution.py:61
  251.6 2.1 subtract_multiply_fusion.4
  253.8 10.5 %fusion.87 = f32[8,3,1024]{2,0,1:T(8,128)S(1)} fusion(f32[3,1024,256]{2,1,0:T(8,128)} %get-tuple-element.423, f32[3,1024,256]{2,1,0:T(8,128)S(1)} %get-tuple-element.424, f32[1024,256]{1,0:T(8,128)} %get-tuple-element.425, f32[3,3]{1,0:T(4,128)S(1)} %fusion.86, f32[8,3,1024]{2,0,1:T(8,128)S(1)} %get-tuple-element.445, pred[]{:T(512)S(6)} %compare.14, ...), kind=kOutput, calls=%fused_computation.13.clone.1 | convolution fusion | flops 233619456 | bytes 7563269 | tf_op jit(solution)/shard_map/while/body/eval_jaxpr/abts,kbs->kat/dot_general | solution.py:61
  266.8 2.1 subtract_multiply_fusion.4
  268.9 10.5 %fusion.87 = f32[8,3,1024]{2,0,1:T(8,128)S(1)} fusion(f32[3,1024,256]{2,1,0:T(8,128)} %get-tuple-element.423, f32[3,1024,256]{2,1,0:T(8,128)S(1)} %get-tuple-element.424, f32[1024,256]{1,0:T(8,128)} %get-tuple-element.425, f32[3,3]{1,0:T(4,128)S(1)} %fusion.86, f32[8,3,1024]{2,0,1:T(8,128)S(1)} %get-tuple-element.445, pred[]{:T(512)S(6)} %compare.14, ...), kind=kOutput, calls=%fused_computation.13.clone.1 | convolution fusion | flops 233619456 | bytes 7563269 | tf_op jit(solution)/shard_map/while/body/eval_jaxpr/abts,kbs->kat/dot_general | solution.py:61
  281.9 2.1 subtract_multiply_fusion.4
  284.0 10.5 %fusion.87 = f32[8,3,1024]{2,0,1:T(8,128)S(1)} fusion(f32[3,1024,256]{2,1,0:T(8,128)} %get-tuple-element.423, f32[3,1024,256]{2,1,0:T(8,128)S(1)} %get-tuple-element.424, f32[1024,256]{1,0:T(8,128)} %get-tuple-element.425, f32[3,3]{1,0:T(4,128)S(1)} %fusion.86, f32[8,3,1024]{2,0,1:T(8,128)S(1)} %get-tuple-element.445, pred[]{:T(512)S(6)} %compare.14, ...), kind=kOutput, calls=%fused_computation.13.clone.1 | convolution fusion | flops 233619456 | bytes 7563269 | tf_op jit(solution)/shard_map/while/body/eval_jaxpr/abts,kbs->kat/dot_general | solution.py:61
  297.0 2.1 subtract_multiply_fusion.4
  299.1 10.5 %fusion.87 = f32[8,3,1024]{2,0,1:T(8,128)S(1)} fusion(f32[3,1024,256]{2,1,0:T(8,128)} %get-tuple-element.423, f32[3,1024,256]{2,1,0:T(8,128)S(1)} %get-tuple-element.424, f32[1024,256]{1,0:T(8,128)} %get-tuple-element.425, f32[3,3]{1,0:T(4,128)S(1)} %fusion.86, f32[8,3,1024]{2,0,1:T(8,128)S(1)} %get-tuple-element.445, pred[]{:T(512)S(6)} %compare.14, ...), kind=kOutput, calls=%fused_computation.13.clone.1 | convolution fusion | flops 233619456 | bytes 7563269 | tf_op jit(solution)/shard_map/while/body/eval_jaxpr/abts,kbs->kat/dot_general | solution.py:61
  312.1 2.1 subtract_multiply_fusion.4
  314.2 10.5 %fusion.87 = f32[8,3,1024]{2,0,1:T(8,128)S(1)} fusion(f32[3,1024,256]{2,1,0:T(8,128)} %get-tuple-element.423, f32[3,1024,256]{2,1,0:T(8,128)S(1)} %get-tuple-element.424, f32[1024,256]{1,0:T(8,128)} %get-tuple-element.425, f32[3,3]{1,0:T(4,128)S(1)} %fusion.86, f32[8,3,1024]{2,0,1:T(8,128)S(1)} %get-tuple-element.445, pred[]{:T(512)S(6)} %compare.14, ...), kind=kOutput, calls=%fused_computation.13.clone.1 | convolution fusion | flops 233619456 | bytes 7563269 | tf_op jit(solution)/shard_map/while/body/eval_jaxpr/abts,kbs->kat/dot_general | solution.py:61
  327.2 2.1 subtract_multiply_fusion.4
  329.4 10.5 %fusion.87 = f32[8,3,1024]{2,0,1:T(8,128)S(1)} fusion(f32[3,1024,256]{2,1,0:T(8,128)} %get-tuple-element.423, f32[3,1024,256]{2,1,0:T(8,128)S(1)} %get-tuple-element.424, f32[1024,256]{1,0:T(8,128)} %get-tuple-element.425, f32[3,3]{1,0:T(4,128)S(1)} %fusion.86, f32[8,3,1024]{2,0,1:T(8,128)S(1)} %get-tuple-element.445, pred[]{:T(512)S(6)} %compare.14, ...), kind=kOutput, calls=%fused_computation.13.clone.1 | convolution fusion | flops 233619456 | bytes 7563269 | tf_op jit(solution)/shard_map/while/body/eval_jaxpr/abts,kbs->kat/dot_general | solution.py:61
  340.6 103.5 %all-reduce.3.cloned.1.call-done = f32[8,3,1024]{2,0,1:T(8,128)} async-done(((f32[8,3,1024]{2,0,1:T(8,128)}), f32[8,3,1024]{2,0,1:T(8,128)}) %all-reduce.3.cloned.1.call-update) | async-done | bytes 98320 | tf_op jit(solution)/shard_map/psum | solution.py:66
  444.9 104.2 %psum.44 = f32[8,8]{0,1:T(8,128)S(1)} all-reduce(f32[8,8]{0,1:T(8,128)S(1)} %convolution_bitcast_fusion.3), channel_id=1, replica_groups=mesh['row'=16,'col'=32] {'row','col'}, use_global_device_ids=true, to_apply=%region_7.10 | all-reduce | flops 64 | bytes 512 | tf_op jit(solution)/shard_map/psum | solution.py:73
  550.1 100.2 %psum.45 = f32[8,8]{0,1:T(8,128)S(1)} all-reduce(f32[8,8]{0,1:T(8,128)S(1)} %convolution_bitcast_fusion.2), channel_id=1, replica_groups=mesh['row'=16,'col'=32] {'row','col'}, use_global_device_ids=true, to_apply=%region_8.11 | all-reduce | flops 64 | bytes 512 | tf_op jit(solution)/shard_map/psum | solution.py:75
  653.5 43.3 %all_gather.15 = f32[8,3,2048]{0,1,2:T(4,128)} all-gather(f32[8,3,64]{0,1,2:T(4,128)S(1)} %copy.44), channel_id=1, replica_groups=mesh['row'=16,'col'=32] {'col'}, dimensions={2}, use_global_device_ids=true | all-gather | bytes 202752 | tf_op jit(solution)/shard_map/all_gather | solution.py:46
  696.8 3.3 copy.45
  700.1 120.9 %while.33 = (s32[]{:T(128)}, f32[8,3,1024]{2,0,1:T(8,128)S(1)}, f32[8,3,2048]{2,0,1:T(8,128)S(1)}, f32[3,1024]{1,0:T(4,128)S(1)}, f32[3,2048]{1,0:T(4,128)S(1)},...) while((s32[]{:T(128)}, f32[8,3,1024]{2,0,1:T(8,128)S(1)}, f32[8,3,2048]{2,0,1:T(8,128)S(1)}, ...), condition=%wide.region_11.14_spmd.clone, body=%wide.region_9.13_spmd.clone.sunk | while | flops 242270240 | bytes 19134656 | solution.py:65
  702.6 2.1 subtract_multiply_fusion.5
  704.8 10.5 %fusion.91 = f32[8,3,1024]{2,0,1:T(8,128)S(1)} fusion(f32[3,1024,256]{2,1,0:T(8,128)} %get-tuple-element.432, f32[3,1024,256]{2,1,0:T(8,128)S(1)} %get-tuple-element.433, f32[1024,256]{1,0:T(8,128)} %get-tuple-element.434, f32[3,3]{1,0:T(4,128)S(1)} %fusion.90, f32[8,3,1024]{2,0,1:T(8,128)S(1)} %get-tuple-element.472, pred[]{:T(512)S(6)} %compare.15, ...), kind=kOutput, calls=%fused_computation.37.clone.1 | convolution fusion | flops 233619456 | bytes 7563269 | tf_op jit(solution)/shard_map/while/body/eval_jaxpr/abts,kbs->kat/dot_general | solution.py:61
  717.8 2.1 subtract_multiply_fusion.5
  719.9 10.5 %fusion.91 = f32[8,3,1024]{2,0,1:T(8,128)S(1)} fusion(f32[3,1024,256]{2,1,0:T(8,128)} %get-tuple-element.432, f32[3,1024,256]{2,1,0:T(8,128)S(1)} %get-tuple-element.433, f32[1024,256]{1,0:T(8,128)} %get-tuple-element.434, f32[3,3]{1,0:T(4,128)S(1)} %fusion.90, f32[8,3,1024]{2,0,1:T(8,128)S(1)} %get-tuple-element.472, pred[]{:T(512)S(6)} %compare.15, ...), kind=kOutput, calls=%fused_computation.37.clone.1 | convolution fusion | flops 233619456 | bytes 7563269 | tf_op jit(solution)/shard_map/while/body/eval_jaxpr/abts,kbs->kat/dot_general | solution.py:61
  732.9 2.1 subtract_multiply_fusion.5
  735.0 10.5 %fusion.91 = f32[8,3,1024]{2,0,1:T(8,128)S(1)} fusion(f32[3,1024,256]{2,1,0:T(8,128)} %get-tuple-element.432, f32[3,1024,256]{2,1,0:T(8,128)S(1)} %get-tuple-element.433, f32[1024,256]{1,0:T(8,128)} %get-tuple-element.434, f32[3,3]{1,0:T(4,128)S(1)} %fusion.90, f32[8,3,1024]{2,0,1:T(8,128)S(1)} %get-tuple-element.472, pred[]{:T(512)S(6)} %compare.15, ...), kind=kOutput, calls=%fused_computation.37.clone.1 | convolution fusion | flops 233619456 | bytes 7563269 | tf_op jit(solution)/shard_map/while/body/eval_jaxpr/abts,kbs->kat/dot_general | solution.py:61
  748.0 2.1 subtract_multiply_fusion.5
  750.1 10.5 %fusion.91 = f32[8,3,1024]{2,0,1:T(8,128)S(1)} fusion(f32[3,1024,256]{2,1,0:T(8,128)} %get-tuple-element.432, f32[3,1024,256]{2,1,0:T(8,128)S(1)} %get-tuple-element.433, f32[1024,256]{1,0:T(8,128)} %get-tuple-element.434, f32[3,3]{1,0:T(4,128)S(1)} %fusion.90, f32[8,3,1024]{2,0,1:T(8,128)S(1)} %get-tuple-element.472, pred[]{:T(512)S(6)} %compare.15, ...), kind=kOutput, calls=%fused_computation.37.clone.1 | convolution fusion | flops 233619456 | bytes 7563269 | tf_op jit(solution)/shard_map/while/body/eval_jaxpr/abts,kbs->kat/dot_general | solution.py:61
  763.1 2.1 subtract_multiply_fusion.5
  765.2 10.5 %fusion.91 = f32[8,3,1024]{2,0,1:T(8,128)S(1)} fusion(f32[3,1024,256]{2,1,0:T(8,128)} %get-tuple-element.432, f32[3,1024,256]{2,1,0:T(8,128)S(1)} %get-tuple-element.433, f32[1024,256]{1,0:T(8,128)} %get-tuple-element.434, f32[3,3]{1,0:T(4,128)S(1)} %fusion.90, f32[8,3,1024]{2,0,1:T(8,128)S(1)} %get-tuple-element.472, pred[]{:T(512)S(6)} %compare.15, ...), kind=kOutput, calls=%fused_computation.37.clone.1 | convolution fusion | flops 233619456 | bytes 7563269 | tf_op jit(solution)/shard_map/while/body/eval_jaxpr/abts,kbs->kat/dot_general | solution.py:61
  778.2 2.1 subtract_multiply_fusion.5
  780.4 10.5 %fusion.91 = f32[8,3,1024]{2,0,1:T(8,128)S(1)} fusion(f32[3,1024,256]{2,1,0:T(8,128)} %get-tuple-element.432, f32[3,1024,256]{2,1,0:T(8,128)S(1)} %get-tuple-element.433, f32[1024,256]{1,0:T(8,128)} %get-tuple-element.434, f32[3,3]{1,0:T(4,128)S(1)} %fusion.90, f32[8,3,1024]{2,0,1:T(8,128)S(1)} %get-tuple-element.472, pred[]{:T(512)S(6)} %compare.15, ...), kind=kOutput, calls=%fused_computation.37.clone.1 | convolution fusion | flops 233619456 | bytes 7563269 | tf_op jit(solution)/shard_map/while/body/eval_jaxpr/abts,kbs->kat/dot_general | solution.py:61
  793.3 2.1 subtract_multiply_fusion.5
  795.5 10.5 %fusion.91 = f32[8,3,1024]{2,0,1:T(8,128)S(1)} fusion(f32[3,1024,256]{2,1,0:T(8,128)} %get-tuple-element.432, f32[3,1024,256]{2,1,0:T(8,128)S(1)} %get-tuple-element.433, f32[1024,256]{1,0:T(8,128)} %get-tuple-element.434, f32[3,3]{1,0:T(4,128)S(1)} %fusion.90, f32[8,3,1024]{2,0,1:T(8,128)S(1)} %get-tuple-element.472, pred[]{:T(512)S(6)} %compare.15, ...), kind=kOutput, calls=%fused_computation.37.clone.1 | convolution fusion | flops 233619456 | bytes 7563269 | tf_op jit(solution)/shard_map/while/body/eval_jaxpr/abts,kbs->kat/dot_general | solution.py:61
  808.4 2.1 subtract_multiply_fusion.5
  810.6 10.5 %fusion.91 = f32[8,3,1024]{2,0,1:T(8,128)S(1)} fusion(f32[3,1024,256]{2,1,0:T(8,128)} %get-tuple-element.432, f32[3,1024,256]{2,1,0:T(8,128)S(1)} %get-tuple-element.433, f32[1024,256]{1,0:T(8,128)} %get-tuple-element.434, f32[3,3]{1,0:T(4,128)S(1)} %fusion.90, f32[8,3,1024]{2,0,1:T(8,128)S(1)} %get-tuple-element.472, pred[]{:T(512)S(6)} %compare.15, ...), kind=kOutput, calls=%fused_computation.37.clone.1 | convolution fusion | flops 233619456 | bytes 7563269 | tf_op jit(solution)/shard_map/while/body/eval_jaxpr/abts,kbs->kat/dot_general | solution.py:61
  821.8 105.6 %all-reduce.5.cloned.1.call-done = f32[8,3,1024]{2,0,1:T(8,128)} async-done(((f32[8,3,1024]{2,0,1:T(8,128)}), f32[8,3,1024]{2,0,1:T(8,128)}) %all-reduce.5.cloned.1.call-update) | async-done | bytes 98320 | tf_op jit(solution)/shard_map/psum | solution.py:66
  929.1 104.0 %psum.47 = f32[8,8]{0,1:T(8,128)S(1)} all-reduce(f32[8,8]{0,1:T(8,128)S(1)} %convolution_bitcast_fusion), channel_id=1, replica_groups=mesh['row'=16,'col'=32] {'row','col'}, use_global_device_ids=true, to_apply=%region_13.16 | all-reduce | flops 64 | bytes 512 | tf_op jit(solution)/shard_map/psum | solution.py:79
  (114 shorter events, 49.1 us)
Async XLA Ops:
  7.2 56.4 %copy-start = (f32[8,3,64]{2,0,1:T(8,128)S(1)}, f32[8,3,64]{2,0,1:T(8,128)}, u32[]{:S(2)}) copy-start(f32[8,3,64]{2,0,1:T(8,128)} %param.10) | copy-start | bytes 18436
  7.2 436.9 %all-reduce.3.cloned.1.call-start = ((), (), s32[]{:S(2)}) async-start(), calls=%async_computation | async-start | bytes 196608 | tf_op jit(solution)/shard_map/psum | solution.py:66
  339.8 0.6 copy-start.3
  340.5 586.9 %all-reduce.5.cloned.1.call-start = ((), (), s32[]{:S(2)}) async-start(), calls=%async_computation.1 | async-start | bytes 196608 | tf_op jit(solution)/shard_map/psum | solution.py:66
  653.4 379.7 %copy-start.1 = (f32[8,3,64]{2,0,1:T(8,128)}, f32[8,3,64]{2,0,1:T(8,128)S(1)}, u32[]{:S(2)}) copy-start(f32[8,3,64]{2,0,1:T(8,128)S(1)} %fusion.61) | copy-start | bytes 18436
  821.0 0.6 copy-start.2
Sparse Core Ops, SparseCore 0:
  340.6 103.3 all-reduce.2
  821.8 105.5 all-reduce.4
where the time goes:
time: 1040 us
  blocking collectives  556 us (53%)
  waiting for transfers between devices  209 us (20%)
  matrix products  173 us (17%)
  other arithmetic  80.1 us (8%)
  between operations  14.1 us (1%)
    psum x2, waiting for transfers between devices, mobility(): summed = lax.psum(partial_image, 'row')  209 us
    dot_general x16, matrix products, add_block(): jnp.einsum('abts,kbs->kat', tensor, block_vectors, precision=lax.Precisio...  168 us
    psum x1, blocking collectives, local(): lax.psum(local_gram(noise, noise), ('row', 'col')) / total_count  104 us
    psum x1, blocking collectives, local(): alpha_one = lax.psum(local_gram(first, image), ('row', 'col')) / total_count  104 us
    psum x1, blocking collectives, local(): alpha_two = lax.psum(local_gram(basis, image), ('row', 'col')) / total_count  104 us
    psum x1, blocking collectives, local(): lax.psum(local_gram(remainder, remainder), ('row', 'col')) / total_count  100 us
    all_gather x2, blocking collectives, mobility(): source_piece = lax.all_gather(vectors, 'col', axis=2, tiled=True)  87.6 us
    all_gather x1, blocking collectives, local(): source_pos = lax.all_gather(positions, 'col', axis=1, tiled=True)  38 us
  transfers between devices with their start and end apart: 2, of which 2 were waited for; matrix products, arithmetic and copies ran while one was open for 0% of the time, Pallas kernels for 0%

commit v1 on v0

--- a/solution.py
+++ b/solution.py
@@ -43,7 +43,9 @@
 
     def mobility(vectors):
         initial = jnp.zeros((vectors.shape[0], 3, target_pos.shape[1]), jnp.float32)
-        source_piece = lax.all_gather(vectors, "col", axis=2, tiled=True)
+        source_piece = jnp.concatenate(
+            lax.all_to_all(jnp.stack([vectors] * lax.axis_size("col")), "col", 0, 0), axis=2
+        )
         piece_width = source_piece.shape[2]
         block_count = 1
         while piece_width % block_count != 0 or piece_width // block_count > 256:

time: 1040 us -> 998 us (0.960)
  blocking collectives: 556 us -> 471 us
  waiting for transfers between devices: 209 us -> 234 us
  starting transfers between devices: 0.08 us -> 17.1 us
    all_gather x2 -> x0, blocking collectives: 87.6 us -> none  [mobility(): source_piece = lax.all_gather(vectors, 'col', axis=2, tiled=True)]
    all_to_all x0 -> x2, waiting for transfers between devices: none -> 18.7 us  [mobility(): lax.all_to_all(jnp.stack([vectors] * lax.axis_size('col')), 'col', 0, 0)]
    all_to_all x0 -> x2, starting transfers between devices: none -> 17 us  [mobility(): lax.all_to_all(jnp.stack([vectors] * lax.axis_size('col')), 'col', 0, 0)]
  transfers between devices with their start and end apart: 2 -> 4, of which waited for: 2 -> 3; matrix products, arithmetic and copies ran while one was open for 0% -> 0% of each run, Pallas kernels for 0% -> 0%
where the time goes in v1:
time: 998 us; the launch traced here: 997 us
  blocking collectives  471 us (47%)
  waiting for transfers between devices  234 us (23%)
  matrix products  173 us (17%)
  other arithmetic  82.3 us (8%)
  starting transfers between devices  17.1 us (2%)
  between operations  14.2 us (1%)
    psum x2, waiting for transfers between devices, mobility(): summed = lax.psum(partial_image, 'row')  215 us
    dot_general x16, matrix products, add_block(): jnp.einsum('abts,kbs->kat', tensor, block_vectors, precision=lax.Precisio...  168 us
    psum x1, blocking collectives, local(): lax.psum(local_gram(noise, noise), ('row', 'col')) / total_count  111 us
    psum x1, blocking collectives, local(): alpha_one = lax.psum(local_gram(first, image), ('row', 'col')) / total_count  104 us
    psum x1, blocking collectives, local(): alpha_two = lax.psum(local_gram(basis, image), ('row', 'col')) / total_count  104 us
    psum x1, blocking collectives, local(): lax.psum(local_gram(remainder, remainder), ('row', 'col')) / total_count  100 us
    all_gather x1, blocking collectives, local(): source_pos = lax.all_gather(positions, 'col', axis=1, tiled=True)  35.8 us
    mul x16, other arithmetic, pair_tensor(): dir_part * displace[:, None] * displace[None, :]  34.2 us
  transfers between devices with their start and end apart: 4, of which 3 were waited for; matrix products, arithmetic and copies ran while one was open for 0% of the time, Pallas kernels for 0%

profile of v1, /device:TPU:1, one launch (start us, length us, event | category | flops | bytes accessed | tf_op | source)
XLA Modules:
  0.0 996.6 jit_solution(16425164572195571710)
XLA Ops:
  8.0 111.0 %psum.42 = f32[8,8]{0,1:T(8,128)S(1)} all-reduce(f32[8,8]{0,1:T(8,128)S(1)} %convolution_bitcast_fusion.5), channel_id=1, replica_groups=mesh['row'=16,'col'=32] {'row','col'}, use_global_device_ids=true, to_apply=%region_0.0 | all-reduce | flops 64 | bytes 512 | tf_op jit(solution)/shard_map/psum | solution.py:71
  123.1 8.4 all-to-all-start
  131.5 35.8 %all-gather.1 = f32[32,64,3]{1,2,0:T(4,128)S(1)} all-gather(f32[1,64,3]{1,2,0:T(4,128)} %bitcast.116), channel_id=1, replica_groups=mesh['row'=16,'col'=32] {'col'}, dimensions={0}, use_global_device_ids=true | all-gather | bytes 25344 | tf_op jit(solution)/shard_map/all_gather | solution.py:42
  167.3 16.0 %all-gather = f32[16,64,3]{1,2,0:T(4,128)S(1)} all-gather(f32[1,64,3]{1,2,0:T(4,128)} %bitcast.117), channel_id=1, replica_groups=mesh['row'=16,'col'=32] {'row'}, dimensions={0}, use_global_device_ids=true | all-gather | bytes 13056 | tf_op jit(solution)/shard_map/all_gather | solution.py:41
  185.4 120.9 %while.32 = (s32[]{:T(128)}, f32[8,3,1024]{2,0,1:T(8,128)S(1)}, f32[8,3,2048]{2,0,1:T(8,128)S(1)}, f32[3,1024]{1,0:T(4,128)S(1)}, f32[3,2048]{1,0:T(4,128)S(1)},...) while((s32[]{:T(128)}, f32[8,3,1024]{2,0,1:T(8,128)S(1)}, f32[8,3,2048]{2,0,1:T(8,128)S(1)}, ...), condition=%wide.region_5.8_spmd.clone, body=%wide.region_3.7_spmd.clone.sunk | while | flops 242270240 | bytes 19134656 | solution.py:67
  185.9 2.0 multiply_select_fusion.4
  187.9 2.1 subtract_multiply_fusion.4
  190.1 10.5 %fusion.87 = f32[8,3,1024]{2,0,1:T(8,128)S(1)} fusion(f32[3,1024,256]{2,1,0:T(8,128)} %get-tuple-element.403, f32[3,1024,256]{2,1,0:T(8,128)S(1)} %get-tuple-element.404, f32[1024,256]{1,0:T(8,128)} %get-tuple-element.405, f32[3,3]{1,0:T(4,128)S(1)} %fusion.86, f32[8,3,1024]{2,0,1:T(8,128)S(1)} %get-tuple-element.425, pred[]{:T(512)S(6)} %compare.14, ...), kind=kOutput, calls=%fused_computation.13.clone.1 | convolution fusion | flops 233619456 | bytes 7563269 | tf_op jit(solution)/shard_map/while/body/eval_jaxpr/abts,kbs->kat/dot_general | solution.py:63
  201.0 2.0 multiply_select_fusion.4
  203.0 2.1 subtract_multiply_fusion.4
  205.2 10.5 %fusion.87 = f32[8,3,1024]{2,0,1:T(8,128)S(1)} fusion(f32[3,1024,256]{2,1,0:T(8,128)} %get-tuple-element.403, f32[3,1024,256]{2,1,0:T(8,128)S(1)} %get-tuple-element.404, f32[1024,256]{1,0:T(8,128)} %get-tuple-element.405, f32[3,3]{1,0:T(4,128)S(1)} %fusion.86, f32[8,3,1024]{2,0,1:T(8,128)S(1)} %get-tuple-element.425, pred[]{:T(512)S(6)} %compare.14, ...), kind=kOutput, calls=%fused_computation.13.clone.1 | convolution fusion | flops 233619456 | bytes 7563269 | tf_op jit(solution)/shard_map/while/body/eval_jaxpr/abts,kbs->kat/dot_general | solution.py:63
  216.2 2.0 multiply_select_fusion.4
  218.2 2.1 subtract_multiply_fusion.4
  220.3 10.5 %fusion.87 = f32[8,3,1024]{2,0,1:T(8,128)S(1)} fusion(f32[3,1024,256]{2,1,0:T(8,128)} %get-tuple-element.403, f32[3,1024,256]{2,1,0:T(8,128)S(1)} %get-tuple-element.404, f32[1024,256]{1,0:T(8,128)} %get-tuple-element.405, f32[3,3]{1,0:T(4,128)S(1)} %fusion.86, f32[8,3,1024]{2,0,1:T(8,128)S(1)} %get-tuple-element.425, pred[]{:T(512)S(6)} %compare.14, ...), kind=kOutput, calls=%fused_computation.13.clone.1 | convolution fusion | flops 233619456 | bytes 7563269 | tf_op jit(solution)/shard_map/while/body/eval_jaxpr/abts,kbs->kat/dot_general | solution.py:63
  233.3 2.1 subtract_multiply_fusion.4
  235.4 10.5 %fusion.87 = f32[8,3,1024]{2,0,1:T(8,128)S(1)} fusion(f32[3,1024,256]{2,1,0:T(8,128)} %get-tuple-element.403, f32[3,1024,256]{2,1,0:T(8,128)S(1)} %get-tuple-element.404, f32[1024,256]{1,0:T(8,128)} %get-tuple-element.405, f32[3,3]{1,0:T(4,128)S(1)} %fusion.86, f32[8,3,1024]{2,0,1:T(8,128)S(1)} %get-tuple-element.425, pred[]{:T(512)S(6)} %compare.14, ...), kind=kOutput, calls=%fused_computation.13.clone.1 | convolution fusion | flops 233619456 | bytes 7563269 | tf_op jit(solution)/shard_map/while/body/eval_jaxpr/abts,kbs->kat/dot_general | solution.py:63
  248.4 2.1 subtract_multiply_fusion.4
  250.5 10.5 %fusion.87 = f32[8,3,1024]{2,0,1:T(8,128)S(1)} fusion(f32[3,1024,256]{2,1,0:T(8,128)} %get-tuple-element.403, f32[3,1024,256]{2,1,0:T(8,128)S(1)} %get-tuple-element.404, f32[1024,256]{1,0:T(8,128)} %get-tuple-element.405, f32[3,3]{1,0:T(4,128)S(1)} %fusion.86, f32[8,3,1024]{2,0,1:T(8,128)S(1)} %get-tuple-element.425, pred[]{:T(512)S(6)} %compare.14, ...), kind=kOutput, calls=%fused_computation.13.clone.1 | convolution fusion | flops 233619456 | bytes 7563269 | tf_op jit(solution)/shard_map/while/body/eval_jaxpr/abts,kbs->kat/dot_general | solution.py:63
  263.5 2.1 subtract_multiply_fusion.4
  265.7 10.5 %fusion.87 = f32[8,3,1024]{2,0,1:T(8,128)S(1)} fusion(f32[3,1024,256]{2,1,0:T(8,128)} %get-tuple-element.403, f32[3,1024,256]{2,1,0:T(8,128)S(1)} %get-tuple-element.404, f32[1024,256]{1,0:T(8,128)} %get-tuple-element.405, f32[3,3]{1,0:T(4,128)S(1)} %fusion.86, f32[8,3,1024]{2,0,1:T(8,128)S(1)} %get-tuple-element.425, pred[]{:T(512)S(6)} %compare.14, ...), kind=kOutput, calls=%fused_computation.13.clone.1 | convolution fusion | flops 233619456 | bytes 7563269 | tf_op jit(solution)/shard_map/while/body/eval_jaxpr/abts,kbs->kat/dot_general | solution.py:63
  278.6 2.1 subtract_multiply_fusion.4
  280.8 10.5 %fusion.87 = f32[8,3,1024]{2,0,1:T(8,128)S(1)} fusion(f32[3,1024,256]{2,1,0:T(8,128)} %get-tuple-element.403, f32[3,1024,256]{2,1,0:T(8,128)S(1)} %get-tuple-element.404, f32[1024,256]{1,0:T(8,128)} %get-tuple-element.405, f32[3,3]{1,0:T(4,128)S(1)} %fusion.86, f32[8,3,1024]{2,0,1:T(8,128)S(1)} %get-tuple-element.425, pred[]{:T(512)S(6)} %compare.14, ...), kind=kOutput, calls=%fused_computation.13.clone.1 | convolution fusion | flops 233619456 | bytes 7563269 | tf_op jit(solution)/shard_map/while/body/eval_jaxpr/abts,kbs->kat/dot_general | solution.py:63
  293.7 2.1 subtract_multiply_fusion.4
  295.9 10.5 %fusion.87 = f32[8,3,1024]{2,0,1:T(8,128)S(1)} fusion(f32[3,1024,256]{2,1,0:T(8,128)} %get-tuple-element.403, f32[3,1024,256]{2,1,0:T(8,128)S(1)} %get-tuple-element.404, f32[1024,256]{1,0:T(8,128)} %get-tuple-element.405, f32[3,3]{1,0:T(4,128)S(1)} %fusion.86, f32[8,3,1024]{2,0,1:T(8,128)S(1)} %get-tuple-element.425, pred[]{:T(512)S(6)} %compare.14, ...), kind=kOutput, calls=%fused_computation.13.clone.1 | convolution fusion | flops 233619456 | bytes 7563269 | tf_op jit(solution)/shard_map/while/body/eval_jaxpr/abts,kbs->kat/dot_general | solution.py:63
  307.0 114.0 %all-reduce.3.cloned.1.call-done = f32[8,3,1024]{2,0,1:T(8,128)} async-done(((f32[8,3,1024]{2,0,1:T(8,128)}), f32[8,3,1024]{2,0,1:T(8,128)}) %all-reduce.3.cloned.1.call-update) | async-done | bytes 98320 | tf_op jit(solution)/shard_map/psum | solution.py:68
  421.9 104.0 %psum.44 = f32[8,8]{0,1:T(8,128)S(1)} all-reduce(f32[8,8]{0,1:T(8,128)S(1)} %convolution_bitcast_fusion.3), channel_id=1, replica_groups=mesh['row'=16,'col'=32] {'row','col'}, use_global_device_ids=true, to_apply=%region_7.10 | all-reduce | flops 64 | bytes 512 | tf_op jit(solution)/shard_map/psum | solution.py:75
  526.9 100.2 %psum.45 = f32[8,8]{0,1:T(8,128)S(1)} all-reduce(f32[8,8]{0,1:T(8,128)S(1)} %convolution_bitcast_fusion.2), channel_id=1, replica_groups=mesh['row'=16,'col'=32] {'row','col'}, use_global_device_ids=true, to_apply=%region_8.11 | all-reduce | flops 64 | bytes 512 | tf_op jit(solution)/shard_map/psum | solution.py:77
  631.1 8.7 all-to-all-start.1
  639.9 18.7 %all-to-all-done.1 = f32[32,1,1536]{2,1,0:T(1,128)S(1)} async-done(((f32[32,1,1536]{2,1,0:T(1,128)}), f32[32,1,1536]{2,1,0:T(1,128)S(1)}, u32[]{:S(2)}, u32[]{:S(2)}) %all-to-all-start.1) | async-done | bytes 196640 | tf_op jit(solution)/shard_map/all_to_all | solution.py:47
  660.1 120.9 %while.33 = (s32[]{:T(128)}, f32[8,3,1024]{2,0,1:T(8,128)S(1)}, f32[8,3,2048]{2,0,1:T(8,128)S(1)}, f32[3,1024]{1,0:T(4,128)S(1)}, f32[3,2048]{1,0:T(4,128)S(1)},...) while((s32[]{:T(128)}, f32[8,3,1024]{2,0,1:T(8,128)S(1)}, f32[8,3,2048]{2,0,1:T(8,128)S(1)}, ...), condition=%wide.region_11.14_spmd.clone, body=%wide.region_9.13_spmd.clone.sunk | while | flops 242270240 | bytes 19134656 | solution.py:67
  662.6 2.1 subtract_multiply_fusion.5
  664.8 10.5 %fusion.91 = f32[8,3,1024]{2,0,1:T(8,128)S(1)} fusion(f32[3,1024,256]{2,1,0:T(8,128)} %get-tuple-element.412, f32[3,1024,256]{2,1,0:T(8,128)S(1)} %get-tuple-element.413, f32[1024,256]{1,0:T(8,128)} %get-tuple-element.414, f32[3,3]{1,0:T(4,128)S(1)} %fusion.90, f32[8,3,1024]{2,0,1:T(8,128)S(1)} %get-tuple-element.452, pred[]{:T(512)S(6)} %compare.15, ...), kind=kOutput, calls=%fused_computation.37.clone.1 | convolution fusion | flops 233619456 | bytes 7563269 | tf_op jit(solution)/shard_map/while/body/eval_jaxpr/abts,kbs->kat/dot_general | solution.py:63
  677.7 2.1 subtract_multiply_fusion.5
  679.9 10.5 %fusion.91 = f32[8,3,1024]{2,0,1:T(8,128)S(1)} fusion(f32[3,1024,256]{2,1,0:T(8,128)} %get-tuple-element.412, f32[3,1024,256]{2,1,0:T(8,128)S(1)} %get-tuple-element.413, f32[1024,256]{1,0:T(8,128)} %get-tuple-element.414, f32[3,3]{1,0:T(4,128)S(1)} %fusion.90, f32[8,3,1024]{2,0,1:T(8,128)S(1)} %get-tuple-element.452, pred[]{:T(512)S(6)} %compare.15, ...), kind=kOutput, calls=%fused_computation.37.clone.1 | convolution fusion | flops 233619456 | bytes 7563269 | tf_op jit(solution)/shard_map/while/body/eval_jaxpr/abts,kbs->kat/dot_general | solution.py:63
  692.9 2.1 subtract_multiply_fusion.5
  695.0 10.5 %fusion.91 = f32[8,3,1024]{2,0,1:T(8,128)S(1)} fusion(f32[3,1024,256]{2,1,0:T(8,128)} %get-tuple-element.412, f32[3,1024,256]{2,1,0:T(8,128)S(1)} %get-tuple-element.413, f32[1024,256]{1,0:T(8,128)} %get-tuple-element.414, f32[3,3]{1,0:T(4,128)S(1)} %fusion.90, f32[8,3,1024]{2,0,1:T(8,128)S(1)} %get-tuple-element.452, pred[]{:T(512)S(6)} %compare.15, ...), kind=kOutput, calls=%fused_computation.37.clone.1 | convolution fusion | flops 233619456 | bytes 7563269 | tf_op jit(solution)/shard_map/while/body/eval_jaxpr/abts,kbs->kat/dot_general | solution.py:63
  708.0 2.1 subtract_multiply_fusion.5
  710.1 10.5 %fusion.91 = f32[8,3,1024]{2,0,1:T(8,128)S(1)} fusion(f32[3,1024,256]{2,1,0:T(8,128)} %get-tuple-element.412, f32[3,1024,256]{2,1,0:T(8,128)S(1)} %get-tuple-element.413, f32[1024,256]{1,0:T(8,128)} %get-tuple-element.414, f32[3,3]{1,0:T(4,128)S(1)} %fusion.90, f32[8,3,1024]{2,0,1:T(8,128)S(1)} %get-tuple-element.452, pred[]{:T(512)S(6)} %compare.15, ...), kind=kOutput, calls=%fused_computation.37.clone.1 | convolution fusion | flops 233619456 | bytes 7563269 | tf_op jit(solution)/shard_map/while/body/eval_jaxpr/abts,kbs->kat/dot_general | solution.py:63
  723.1 2.1 subtract_multiply_fusion.5
  725.2 10.5 %fusion.91 = f32[8,3,1024]{2,0,1:T(8,128)S(1)} fusion(f32[3,1024,256]{2,1,0:T(8,128)} %get-tuple-element.412, f32[3,1024,256]{2,1,0:T(8,128)S(1)} %get-tuple-element.413, f32[1024,256]{1,0:T(8,128)} %get-tuple-element.414, f32[3,3]{1,0:T(4,128)S(1)} %fusion.90, f32[8,3,1024]{2,0,1:T(8,128)S(1)} %get-tuple-element.452, pred[]{:T(512)S(6)} %compare.15, ...), kind=kOutput, calls=%fused_computation.37.clone.1 | convolution fusion | flops 233619456 | bytes 7563269 | tf_op jit(solution)/shard_map/while/body/eval_jaxpr/abts,kbs->kat/dot_general | solution.py:63
  738.2 2.1 subtract_multiply_fusion.5
  740.3 10.5 %fusion.91 = f32[8,3,1024]{2,0,1:T(8,128)S(1)} fusion(f32[3,1024,256]{2,1,0:T(8,128)} %get-tuple-element.412, f32[3,1024,256]{2,1,0:T(8,128)S(1)} %get-tuple-element.413, f32[1024,256]{1,0:T(8,128)} %get-tuple-element.414, f32[3,3]{1,0:T(4,128)S(1)} %fusion.90, f32[8,3,1024]{2,0,1:T(8,128)S(1)} %get-tuple-element.452, pred[]{:T(512)S(6)} %compare.15, ...), kind=kOutput, calls=%fused_computation.37.clone.1 | convolution fusion | flops 233619456 | bytes 7563269 | tf_op jit(solution)/shard_map/while/body/eval_jaxpr/abts,kbs->kat/dot_general | solution.py:63
  753.3 2.1 subtract_multiply_fusion.5
  755.5 10.5 %fusion.91 = f32[8,3,1024]{2,0,1:T(8,128)S(1)} fusion(f32[3,1024,256]{2,1,0:T(8,128)} %get-tuple-element.412, f32[3,1024,256]{2,1,0:T(8,128)S(1)} %get-tuple-element.413, f32[1024,256]{1,0:T(8,128)} %get-tuple-element.414, f32[3,3]{1,0:T(4,128)S(1)} %fusion.90, f32[8,3,1024]{2,0,1:T(8,128)S(1)} %get-tuple-element.452, pred[]{:T(512)S(6)} %compare.15, ...), kind=kOutput, calls=%fused_computation.37.clone.1 | convolution fusion | flops 233619456 | bytes 7563269 | tf_op jit(solution)/shard_map/while/body/eval_jaxpr/abts,kbs->kat/dot_general | solution.py:63
  768.4 2.1 subtract_multiply_fusion.5
  770.6 10.5 %fusion.91 = f32[8,3,1024]{2,0,1:T(8,128)S(1)} fusion(f32[3,1024,256]{2,1,0:T(8,128)} %get-tuple-element.412, f32[3,1024,256]{2,1,0:T(8,128)S(1)} %get-tuple-element.413, f32[1024,256]{1,0:T(8,128)} %get-tuple-element.414, f32[3,3]{1,0:T(4,128)S(1)} %fusion.90, f32[8,3,1024]{2,0,1:T(8,128)S(1)} %get-tuple-element.452, pred[]{:T(512)S(6)} %compare.15, ...), kind=kOutput, calls=%fused_computation.37.clone.1 | convolution fusion | flops 233619456 | bytes 7563269 | tf_op jit(solution)/shard_map/while/body/eval_jaxpr/abts,kbs->kat/dot_general | solution.py:63
  781.8 100.8 %all-reduce.5.cloned.1.call-done = f32[8,3,1024]{2,0,1:T(8,128)} async-done(((f32[8,3,1024]{2,0,1:T(8,128)}), f32[8,3,1024]{2,0,1:T(8,128)}) %all-reduce.5.cloned.1.call-update) | async-done | bytes 98320 | tf_op jit(solution)/shard_map/psum | solution.py:68
  884.3 104.0 %psum.47 = f32[8,8]{0,1:T(8,128)S(1)} all-reduce(f32[8,8]{0,1:T(8,128)S(1)} %convolution_bitcast_fusion), channel_id=1, replica_groups=mesh['row'=16,'col'=32] {'row','col'}, use_global_device_ids=true, to_apply=%region_13.16 | all-reduce | flops 64 | bytes 512 | tf_op jit(solution)/shard_map/psum | solution.py:81
  (127 shorter events, 52.9 us)
Async XLA Ops:
  7.2 0.7 copy-start
  123.1 60.3 %all-to-all-start = ((f32[32,1,1536]{2,1,0:T(1,128)}), f32[32,1,1536]{2,1,0:T(1,128)S(1)}, u32[]{:S(2)}, u32[]{:S(2)}) async-start(f32[32,1,1536]{2,1,0:T(1,128)} %reshape.149), calls=%async_computation | async-start | bytes 393216 | tf_op jit(solution)/shard_map/all_to_all | solution.py:47
  131.4 289.6 %all-reduce.3.cloned.1.call-start = ((), (), s32[]{:S(2)}) async-start(), calls=%async_computation.2 | async-start | bytes 196608 | tf_op jit(solution)/shard_map/psum | solution.py:68
  306.4 0.6 copy-start.2
  630.2 358.1 %copy-start.1 = (f32[8,3,64]{2,0,1:T(8,128)}, f32[8,3,64]{2,0,1:T(8,128)S(1)}, u32[]{:S(2)}) copy-start(f32[8,3,64]{2,0,1:T(8,128)S(1)} %fusion.61) | copy-start | bytes 18436
  631.1 27.5 %all-to-all-start.1 = ((f32[32,1,1536]{2,1,0:T(1,128)}), f32[32,1,1536]{2,1,0:T(1,128)S(1)}, u32[]{:S(2)}, u32[]{:S(2)}) async-start(f32[32,1,1536]{2,1,0:T(1,128)} %reshape.151), calls=%async_computation.1 | async-start | bytes 393216 | tf_op jit(solution)/shard_map/all_to_all | solution.py:47
  639.8 242.8 %all-reduce.5.cloned.1.call-start = ((), (), s32[]{:S(2)}) async-start(), calls=%async_computation.3 | async-start | bytes 196608 | tf_op jit(solution)/shard_map/psum | solution.py:68
  781.0 0.6 copy-start.3
Sparse Core Ops, SparseCore 0:
  307.1 113.8 all-reduce.2
  781.8 100.7 all-reduce.4
